TPU v7x, 32 devices: a whole 2x2x4 slice. The times are simulated.
32 devices in a mesh: dp: 32 (over z, y, x, core).
Axes of the slice: x: 2, y: 2, z: 4, core: 2. Of those that a mesh axis runs over, the one named last changes fastest.
Arguments:
- block_input: bfloat16 [4096, 1088], P('dp'), may hold values from -6 to 6
- out_cotangent: bfloat16 [4096, 1088], P('dp'), may hold values from -6 to 6
- seq_lengths: int32 [32, 4], P('dp'), may hold values from 1 to 64, 128 in all within a row
- w_qkv: bfloat16 [3551232], P('dp'), may hold values from -1 to 1
- w_out: bfloat16 [1183744], P('dp'), may hold values from -0.75 to 0.75
- w_up: bfloat16 [4734976], P('dp'), may hold values from -0.1875 to 0.1875
- w_down: bfloat16 [4734976], P('dp'), may hold values from -0.09375 to 0.09375
- vectors: bfloat16 [13056], P('dp'), may hold values from 0.099609375 to 1.8984375
Outputs:
- block_output: bfloat16 [4096, 1088], P('dp')
- input_grad: float32 [4096, 1088], P('dp')
- grad_qkv: float32 [3551232], P('dp')
- grad_out: float32 [1183744], P('dp')
- grad_up: float32 [4734976], P('dp')
- grad_down: float32 [4734976], P('dp')
- grad_vectors: float32 [13056], P('dp')
Inputs may be any that keep to these rules, and one draw needn't show every extreme that they name: `seq_lengths`: in every row the lengths sum to 128; the longest sequence has 64 tokens.
All inputs are finite; a program needn't handle non-finite values.
Results may differ from a plain program's by a relative error of at most 0.012.
The roundings to bfloat16 on the way count: a program that leaves them out, or rounds other values in their place, can miss the bound.
Values may be sent and summed in bfloat16 or wider, within the bound.
A program may use at most 320 MiB of HBM per device.

v0:
```python
import jax
import jax.numpy as jnp
from jax import lax
from jax.sharding import PartitionSpec as P

HEADS = 17
HEAD_DIM = 64


EPS = 1e-05
ROOT_HALF = 0.7071067811865476
INV_ROOT_TAU = 0.3989422804014327


def layer_norm(rows, gain, shift):
    mean = jnp.mean(rows, axis=1, keepdims=True)
    centered = rows - mean
    inverse = lax.rsqrt(jnp.mean(centered * centered, axis=1, keepdims=True) + EPS)
    normed = centered * inverse
    return (normed, inverse, normed * gain + shift)


def norm_back(grad_rows, normed, inverse, gain):
    scaled = grad_rows * gain
    inner = jnp.mean(scaled * normed, axis=1, keepdims=True)
    return inverse * (scaled - jnp.mean(scaled, axis=1, keepdims=True) - normed * inner)


def gelu_exact(value):
    return 0.5 * value * (1.0 + lax.erf(value * ROOT_HALF))


def gelu_slope(value):
    return (
        0.5 * (1.0 + lax.erf(value * ROOT_HALF))
        + value * jnp.exp(-0.5 * value * value) * INV_ROOT_TAU
    )


def causal_mask(lengths, rows):
    ends = jnp.cumsum(lengths)
    position = jnp.arange(rows, dtype=jnp.int32)
    segment = jnp.sum((position[:, None] >= ends[None, :]).astype(jnp.int32), axis=1)
    return (segment[:, None] == segment[None, :]) & (position[None, :] <= position[:, None])


def score_block(query, keys, mask):
    scores = jnp.einsum("qhe,khe->hqk", query, keys, preferred_element_type=jnp.float32)
    return jnp.where(mask[None], scores, -1e30)


def shape_params(flat_parts, width):
    hidden = 4 * width
    return (
        flat_parts[0].reshape(width, 3 * width),
        flat_parts[1].reshape(width, width),
        flat_parts[2].reshape(width, hidden),
        flat_parts[3].reshape(hidden, width),
        flat_parts[4].astype(jnp.float32),
    )


def window_term(left_rows, right_rows, flat_start, flat_count):
    inner_len = left_rows.shape[1]
    columns = right_rows.shape[1]
    row_count = min(inner_len, flat_count // columns + 2)
    row_first = jnp.clip(flat_start // columns, 0, inner_len - row_count)
    product = lax.dot_general(
        left_rows, right_rows, (((0,), (0,)), ((), ())), preferred_element_type=jnp.float32
    ).reshape(-1)
    padded = jnp.concatenate([product, jnp.zeros((flat_count,), jnp.float32)])
    return lax.dynamic_slice_in_dim(padded, flat_start - row_first * columns, flat_count, 0)


def shard_terms(pairs, vector_grad, device_total):
    piece_lens = [
        left_rows.shape[1] * right_rows.shape[1] // device_total for left_rows, right_rows in pairs
    ]
    piece_lens = piece_lens + [vector_grad.shape[0] // device_total]
    shard_len = sum(piece_lens)

    def shard_term(start, count):
        dev_count = count // shard_len
        dev_first = start // shard_len
        pieces = []
        for (left_rows, right_rows), piece_len in zip(pairs, piece_lens):
            window = window_term(
                left_rows, right_rows, dev_first * piece_len, dev_count * piece_len
            )
            pieces.append(window.reshape(dev_count, piece_len))
        vec_len = piece_lens[-1]
        window = vector_grad
        pieces.append(window.reshape(dev_count, vec_len))
        return jnp.concatenate(pieces, axis=1).reshape(-1)

    return (shard_term, shard_len, piece_lens)


def split_shard(summed, piece_lens):
    outputs = []
    offset = 0
    for piece_len in piece_lens:
        outputs.append(summed[offset : offset + piece_len])
        offset = offset + piece_len
    return outputs


def body(block_input, out_cotangent, seq_lengths, w_qkv, w_out, w_up, w_down, vectors):
    rows, width = block_input.shape
    hidden = 4 * width
    scale = HEAD_DIM ** (-0.5)
    device_total = lax.axis_size("dp")
    mask = causal_mask(seq_lengths[0], rows)
    fetched = (
        lax.all_gather(w_qkv, "dp", axis=0, tiled=True),
        lax.all_gather(w_out, "dp", axis=0, tiled=True),
        lax.all_gather(w_up, "dp", axis=0, tiled=True),
        lax.all_gather(w_down, "dp", axis=0, tiled=True),
        lax.all_gather(vectors, "dp", axis=0, tiled=True),
    )
    wqkv, wo, wup, wdn, vec = shape_params(fetched, width)
    inputs = block_input.astype(jnp.float32)
    normed1, inverse1, pre1 = layer_norm(inputs, vec[0:width], vec[width : 2 * width])
    first = pre1.astype(jnp.bfloat16)
    qkv = jnp.dot(first, wqkv, preferred_element_type=jnp.float32)
    query = (
        ((qkv[:, 0:width] + vec[2 * width : 3 * width]) * scale)
        .astype(jnp.bfloat16)
        .reshape(rows, HEADS, HEAD_DIM)
    )
    keys = qkv[:, width : 2 * width].astype(jnp.bfloat16).reshape(rows, HEADS, HEAD_DIM)
    values = (
        (qkv[:, 2 * width : 3 * width] + vec[3 * width : 4 * width])
        .astype(jnp.bfloat16)
        .reshape(rows, HEADS, HEAD_DIM)
    )
    scores = score_block(query, keys, mask)
    peak = jnp.max(scores, axis=2, keepdims=True)
    logsum = peak + jnp.log(jnp.sum(jnp.exp(scores - peak), axis=2, keepdims=True))
    probs_low = jnp.exp(scores - logsum).astype(jnp.bfloat16)
    mixed = jnp.einsum("hqk,khe->qhe", probs_low, values, preferred_element_type=jnp.float32)
    mixed = mixed.astype(jnp.bfloat16).reshape(rows, width)
    resid = (
        inputs + jnp.dot(mixed, wo, preferred_element_type=jnp.float32) + vec[4 * width : 5 * width]
    )
    normed2, inverse2, pre2 = layer_norm(
        resid, vec[5 * width : 6 * width], vec[6 * width : 7 * width]
    )
    second = pre2.astype(jnp.bfloat16)
    upper = (
        jnp.dot(second, wup, preferred_element_type=jnp.float32)
        + vec[7 * width : 7 * width + hidden]
    )
    active = gelu_exact(upper).astype(jnp.bfloat16)
    output = (
        resid + jnp.dot(active, wdn, preferred_element_type=jnp.float32) + vec[7 * width + hidden :]
    )
    block_output = output.astype(jnp.bfloat16)
    back_w = (wqkv, wo, wup, wdn)
    bqkv, bwo, bwup, bwdn = back_w
    grad_top = out_cotangent.astype(jnp.float32)
    d_upper = jnp.dot(out_cotangent, bwdn.T, preferred_element_type=jnp.float32) * gelu_slope(upper)
    d_upper_low = d_upper.astype(jnp.bfloat16)
    d_second = jnp.dot(d_upper_low, bwup.T, preferred_element_type=jnp.float32)
    d_resid = grad_top + norm_back(d_second, normed2, inverse2, vec[5 * width : 6 * width])
    d_resid_low = d_resid.astype(jnp.bfloat16)
    d_mixed = jnp.dot(d_resid_low, bwo.T, preferred_element_type=jnp.float32).astype(jnp.bfloat16)
    d_mixed = d_mixed.reshape(rows, HEADS, HEAD_DIM)
    probs = jnp.exp(score_block(query, keys, mask) - logsum)
    probs_low = probs.astype(jnp.bfloat16)
    d_values = jnp.einsum("hqk,qhe->khe", probs_low, d_mixed, preferred_element_type=jnp.float32)
    d_probs = jnp.einsum("qhe,khe->hqk", d_mixed, values, preferred_element_type=jnp.float32)
    delta = jnp.sum(probs * d_probs, axis=2, keepdims=True)
    d_scores = (probs * (d_probs - delta)).astype(jnp.bfloat16)
    d_query = (
        jnp.einsum("hqk,khe->qhe", d_scores, keys, preferred_element_type=jnp.float32).reshape(
            rows, width
        )
        * scale
    )
    d_keys = jnp.einsum(
        "hqk,qhe->khe", d_scores, query, preferred_element_type=jnp.float32
    ).reshape(rows, width)
    d_values = d_values.reshape(rows, width)
    d_qkv = jnp.concatenate([d_query, d_keys, d_values], axis=1).astype(jnp.bfloat16)
    d_first = jnp.dot(d_qkv, bqkv.T, preferred_element_type=jnp.float32)
    input_grad = d_resid + norm_back(d_first, normed1, inverse1, vec[0:width])
    g_vec = jnp.concatenate(
        [
            jnp.sum(d_first * normed1, axis=0),
            jnp.sum(d_first, axis=0),
            jnp.sum(d_query, axis=0),
            jnp.sum(d_values, axis=0),
            jnp.sum(d_resid, axis=0),
            jnp.sum(d_second * normed2, axis=0),
            jnp.sum(d_second, axis=0),
            jnp.sum(d_upper, axis=0),
            jnp.sum(grad_top, axis=0),
        ]
    )
    all_term, all_len, all_lens = shard_terms(
        [(first, d_qkv), (mixed, d_resid_low), (second, d_upper_low), (active, out_cotangent)],
        g_vec,
        device_total,
    )
    grad_qkv, grad_out, grad_up, grad_down, grad_vectors = split_shard(
        lax.psum_scatter(
            all_term(jnp.int32(0), all_len * lax.axis_size("dp")),
            "dp",
            scatter_dimension=0,
            tiled=True,
        ),
        all_lens,
    )
    return (block_output, input_grad, grad_qkv, grad_out, grad_up, grad_down, grad_vectors)


def solution(mesh):
    in_specs = (
        P("dp", None),
        P("dp", None),
        P("dp", None),
        P("dp"),
        P("dp"),
        P("dp"),
        P("dp"),
        P("dp"),
    )
    out_specs = (P("dp", None), P("dp", None), P("dp"), P("dp"), P("dp"), P("dp"), P("dp"))
    return jax.shard_map(body, mesh=mesh, in_specs=in_specs, out_specs=out_specs, check_vma=False)
```

profile of v0, /device:TPU:0, one launch (start us, length us, event | category | flops | bytes accessed | tf_op | source)
XLA Modules:
  0.0 1735.4 jit_solution(6460732507274174659)
XLA Ops:
  7.2 1.7 reshape.223
  9.0 2.0 reshape.221
  11.0 4.4 reshape.227
  15.5 4.1 reshape.225
  19.9 42.8 %all-reduce = bf16[13056]{0:T(1024)(128)(2,1)S(1)} all-reduce(bf16[13056]{0:T(1024)(128)(2,1)S(1)} %dynamic-update-slice), channel_id=1, replica_groups=mesh['dp'=32] {'dp'}, use_global_device_ids=true, to_apply=%add | all-reduce | flops 13056 | bytes 52224
  63.6 0.7 fusion.47
  64.2 13.6 all-gather.11.cloned.1.call-done
  77.9 50.8 %reduce.4 = bf16[32,36992]{1,0:T(8,128)(2,1)} reduce(bf16[32,1,36992]{2,1,0:T(2,128)(2,1)} %all-gather.11.cloned.1.call-done, bf16[]{:T(256)} %constant.148), dimensions={1}, to_apply=%all-gather.1.reduce_sub_computation | reduce | bytes 4734978 | tf_op jit(solution)/shard_map/all_gather | solution.py:116
  128.7 5.1 reshape.211
  133.8 49.1 %all-gather.9.cloned.1.call-done = bf16[32,1,110976]{2,1,0:T(2,128)(2,1)} async-done(((bf16[1,1,110976]{2,1,0:T(2,128)(2,1)}), bf16[32,1,110976]{2,1,0:T(2,128)(2,1)}) %all-gather.9.cloned.1.call-update) | async-done | bytes 7102480 | tf_op jit(solution)/shard_map/all_gather | solution.py:115
  182.8 130.2 %reduce.3 = bf16[32,110976]{1,0:T(8,128)(2,1)} reduce(bf16[32,1,110976]{2,1,0:T(2,128)(2,1)} %all-gather.9.cloned.1.call-done, bf16[]{:T(256)} %constant.148), dimensions={1}, to_apply=%all-gather.reduce_sub_computation | reduce | bytes 14204930 | tf_op jit(solution)/shard_map/all_gather | solution.py:115
  313.1 9.7 reshape.204
  322.8 6.4 fusion.40
  330.5 0.9 copy-done
  331.4 1.2 fusion.49
  332.8 156.2 %reduce.6 = bf16[32,147968]{1,0:T(8,128)(2,1)} reduce(bf16[32,1,147968]{2,1,0:T(2,128)(2,1)} %all-gather.15.cloned.1.call-done, bf16[]{:T(256)} %constant.148), dimensions={1}, to_apply=%all-gather.3.reduce_sub_computation | reduce | bytes 18939906 | tf_op jit(solution)/shard_map/all_gather | solution.py:118
  488.9 11.8 reshape.213
  500.8 155.9 %reduce.5 = bf16[32,147968]{1,0:T(8,128)(2,1)} reduce(bf16[32,1,147968]{2,1,0:T(2,128)(2,1)} %all-gather.13.cloned.1.call-done, bf16[]{:T(256)} %constant.148), dimensions={1}, to_apply=%all-gather.2.reduce_sub_computation | reduce | bytes 18939906 | tf_op jit(solution)/shard_map/all_gather | solution.py:117
  656.7 17.6 %reshape.212 = bf16[1088,4352]{1,0:T(8,128)(2,1)} reshape(bf16[32,147968]{1,0:T(8,128)(2,1)} %reduce.5) | data formatting | bytes 18939904 | tf_op jit(solution)/shard_map/reshape | solution.py:57
  674.4 5.6 convolution_add_fusion
  680.1 7.6 fusion.50
  687.7 2.8 multiply_reduce_fusion.1
  691.0 0.8 convolution_convert_fusion
  691.9 0.6 fusion.45
  694.6 2.2 fusion.20
  696.7 7.6 fusion.29
  704.3 3.0 fusion.33
  707.4 8.0 fusion.25
  715.4 8.3 fusion.42
  723.7 14.5 dynamic_slice.12
  738.1 11.1 constant_dynamic-update-slice_fusion.4
  749.3 6.4 dynamic_slice.13
  755.7 23.9 %dynamic_slice.14 = f32[32,147968]{1,0:T(8,128)} reshape(f32[1088,4352]{1,0:T(8,128)} %fusion.25) | data formatting | bytes 37879808 | tf_op jit(solution)/shard_map/dynamic_slice | solution.py:72
  779.6 24.6 %dynamic_slice.15 = f32[32,147968]{1,0:T(8,128)} reshape(f32[4352,1088]{1,0:T(8,128)} %fusion.42) | data formatting | bytes 37879808 | tf_op jit(solution)/shard_map/dynamic_slice | solution.py:72
  804.6 5.2 constant_dynamic-update-slice_fusion.3
  809.8 14.6 constant_dynamic-update-slice_fusion.2
  824.4 1.3 slice-done.6
  825.8 0.6 slice-done.7
  826.4 7.3 constant_dynamic-update-slice_fusion.1
  833.6 0.6 constant_dynamic-update-slice_fusion
  834.3 80.8 %reshape.218 = f32[14217984]{0:T(1024)} reshape(f32[32,444312]{1,0:T(8,128)} %constant_dynamic-update-slice_fusion) | data formatting | bytes 113743872 | tf_op jit(solution)/shard_map/reshape | solution.py:94
  915.2 1.0 fusion.19
  916.2 10.1 fusion.2
  926.3 794.7 %all-reduce.4.cloned.1.call-done = f32[14217984]{0:T(1024)} async-done(((f32[14217984]{0:T(1024)}), f32[14217984]{0:T(1024)}) %all-reduce.4.cloned.1.call-update) | async-done | bytes 56871952
  1721.0 2.0 dynamic-slice.1
  1722.9 1.7 dynamic-slice.2
  1724.6 1.3 dynamic-slice.5
  1726.0 2.6 fusion.44
  (87 shorter events, 5.7 us)
Async XLA Ops:
  7.2 8.3 copy-start.8
  7.2 12.5 copy-start.10
  7.2 70.7 %all-gather.11.cloned.1.call-start = ((), (), s32[]{:S(2)}) async-start(), calls=%async_computation.1 | async-start | bytes 4882944 | tf_op jit(solution)/shard_map/all_gather | solution.py:116
  8.9 54.0 %copy-start.11 = (s32[1,4]{1,0:T(1,128)S(1)}, s32[1,4]{1,0:T(1,128)}, u32[]{:S(2)}) copy-start(s32[1,4]{1,0:T(1,128)} %param.10) | copy-start | bytes 52
  8.9 54.2 %copy-start.3 = (bf16[128,1088]{0,1:T(8,128)(2,1)S(1)}, bf16[128,1088]{0,1:T(8,128)(2,1)}, u32[]{:S(2)}) copy-start(bf16[128,1088]{0,1:T(8,128)(2,1)} %param.8) | copy-start | bytes 835588
  8.9 173.9 %all-gather.9.cloned.1.call-start = ((), (), s32[]{:S(2)}) async-start(), calls=%async_computation | async-start | bytes 14648832 | tf_op jit(solution)/shard_map/all_gather | solution.py:115
  11.0 321.8 %all-gather.15.cloned.1.call-start = ((), (), s32[]{:S(2)}) async-start(), calls=%async_computation.3 | async-start | bytes 19531776 | tf_op jit(solution)/shard_map/all_gather | solution.py:118
  15.4 485.3 %all-gather.13.cloned.1.call-start = ((), (), s32[]{:S(2)}) async-start(), calls=%async_computation.2 | async-start | bytes 19531776 | tf_op jit(solution)/shard_map/all_gather | solution.py:117
  19.6 1701.4 %all-reduce.4.cloned.1.call-start = ((), (), s32[]{:S(2)}) async-start(), calls=%async_computation.4 | async-start | bytes 113745920
  329.6 0.9 copy-start.4
  329.6 1.8 copy-start
  674.4 5.7 copy-start.6
  674.4 13.3 slice-start
  674.4 13.3 slice-start.1
  680.0 35.3 %copy-start.2 = (f32[128,4352]{1,0:T(8,128)}, f32[128,4352]{1,0:T(8,128)S(1)}, u32[]{:S(2)}) copy-start(f32[128,4352]{1,0:T(8,128)S(1)} %convolution_add_fusion) | copy-start | bytes 6684676
  680.0 7.6 slice-start.2
  687.7 3.3 copy-start.1
  691.0 1.5 copy-start.5
  691.0 3.0 slice-start.8
  692.5 2.1 slice-start.9
  707.4 8.0 copy-start.7
  804.5 19.9 %slice-start.3 = ((s8[18939904]{0:T(1024)(128)(4,1)}), s8[4194304]{0:T(1024)(128)(4,1)S(1)}, s32[]{:S(2)}) async-start(s8[18939904]{0:T(1024)(128)(4,1)} %bitcast.44), calls=%async_computation.8 | async-start | bytes 8388608
  804.6 19.9 %slice-start.4 = ((s8[18939904]{0:T(1024)(128)(4,1)}), s8[4194304]{0:T(1024)(128)(4,1)S(1)}, s32[]{:S(2)}) async-start(s8[18939904]{0:T(1024)(128)(4,1)} %bitcast.44), calls=%async_computation.9 | async-start | bytes 8388608
  809.8 14.6 slice-start.5
  809.8 16.0 slice-start.6
  809.8 16.6 slice-start.7
  915.1 1.1 copy-start.9
Sparse Core Ops, SparseCore 0:
  11.5 66.3 all-gather.10
  81.3 101.4 all-gather.8
  186.3 122.6 all-gather.14
  312.4 122.4 all-gather.12
  915.3 805.6 all-reduce.3
where the time goes:
time: 1740 us
  waiting for transfers between devices  858 us (49%)
  other arithmetic  496 us (29%)
  local copies, waits for them, and re-layouts  258 us (15%)
  matrix products  66.1 us (4%)
  blocking collectives  42.8 us (2%)
    unnamed x6, waiting for transfers between devices  795 us
    all_gather x1, other arithmetic, body(): lax.all_gather(w_down, 'dp', axis=0, tiled=True)  156 us
    all_gather x1, other arithmetic, body(): lax.all_gather(w_up, 'dp', axis=0, tiled=True)  156 us
    all_gather x1, other arithmetic, body(): lax.all_gather(w_qkv, 'dp', axis=0, tiled=True)  130 us
    reshape x1, local copies, waits for them, and re-layouts, shard_term(): return jnp.concatenate(pieces, axis=1).reshape(-1)  80.8 us
    dynamic_slice x4, local copies, waits for them, and re-layouts, window_term(): lax.dynamic_slice_in_dim(padded, flat_start - row_first * columns, flat_c...  69.4 us
    unnamed x54, local copies, waits for them, and re-layouts  54.1 us
    all_gather x1, other arithmetic, body(): lax.all_gather(w_out, 'dp', axis=0, tiled=True)  50.8 us
  transfers between devices with their start and end apart: 5, of which 3 were waited for; matrix products, arithmetic and copies ran while one was open for 23% of the time, Pallas kernels for 0%

commit v1 on v0

--- a/solution.py
+++ b/solution.py
@@ -105,20 +105,86 @@
     return outputs
 
 
+def fetch_flat(w_qkv, w_out, w_up, w_down, vectors, width):
+    fetched = tuple(
+        lax.all_gather(part, "dp", axis=0, tiled=True)
+        for part in (w_qkv, w_out, w_up, w_down, vectors)
+    )
+    return shape_params(fetched, width)
+
+
+def reduce_flat(pairs, g_vec, device_total):
+    all_term, all_len, all_lens = shard_terms(pairs, g_vec, device_total)
+    return split_shard(
+        lax.psum_scatter(
+            all_term(jnp.int32(0), all_len * device_total),
+            "dp",
+            scatter_dimension=0,
+            tiled=True,
+        ),
+        all_lens,
+    )
+
+
+def fetch_rows(w_qkv, w_out, w_up, w_down, vectors, width, total):
+    own = width // total
+    count = vectors.shape[0]
+    side = jnp.concatenate([w_qkv.reshape(own, 3 * width), w_out.reshape(own, width)], axis=1)
+    extra = jnp.pad(vectors, (0, 4 * width - count)).reshape(1, 4 * width)
+    side = lax.all_gather(jnp.concatenate([side, extra], axis=0), "dp", axis=0, tiled=False)
+    wup = lax.all_gather(w_up.reshape(own, 4 * width), "dp", axis=0, tiled=False)
+    wdn = lax.all_gather(w_down.reshape(4 * own, width), "dp", axis=0, tiled=True)
+    both = side[:, :own].reshape(width, 4 * width)
+    vec = side[:, own, :count].reshape(-1).astype(jnp.float32)
+    return both[:, : 3 * width], both[:, 3 * width :], wup.reshape(width, 4 * width), wdn, vec
+
+
+def product_low(left_rows, right_rows):
+    return lax.dot_general(
+        left_rows, right_rows, (((0,), (0,)), ((), ())), preferred_element_type=jnp.float32
+    ).astype(jnp.bfloat16)
+
+
+def reduce_rows(pairs, g_vec, total):
+    width = pairs[0][0].shape[1]
+    own = width // total
+    count = g_vec.shape[0] // total
+    low = [product_low(left, right) for left, right in pairs]
+    down = lax.psum_scatter(low[3], "dp", scatter_dimension=0, tiled=True)
+    up = lax.psum_scatter(
+        low[2].reshape(total, own, 4 * width), "dp", scatter_dimension=0, tiled=False
+    )
+    side = jnp.concatenate([low[0], low[1]], axis=1).reshape(total, own, 4 * width)
+    extra = jnp.pad(
+        g_vec.reshape(total, 1, count).astype(jnp.bfloat16),
+        ((0, 0), (0, 0), (0, 4 * width - count)),
+    )
+    side = lax.psum_scatter(
+        jnp.concatenate([side, extra], axis=1), "dp", scatter_dimension=0, tiled=False
+    )
+    parts = (
+        side[:own, : 3 * width],
+        side[:own, 3 * width :],
+        up,
+        down,
+        side[own, :count],
+    )
+    return [part.astype(jnp.float32).reshape(-1) for part in parts]
+
+
 def body(block_input, out_cotangent, seq_lengths, w_qkv, w_out, w_up, w_down, vectors):
     rows, width = block_input.shape
     hidden = 4 * width
     scale = HEAD_DIM ** (-0.5)
     device_total = lax.axis_size("dp")
     mask = causal_mask(seq_lengths[0], rows)
-    fetched = (
-        lax.all_gather(w_qkv, "dp", axis=0, tiled=True),
-        lax.all_gather(w_out, "dp", axis=0, tiled=True),
-        lax.all_gather(w_up, "dp", axis=0, tiled=True),
-        lax.all_gather(w_down, "dp", axis=0, tiled=True),
-        lax.all_gather(vectors, "dp", axis=0, tiled=True),
-    )
-    wqkv, wo, wup, wdn, vec = shape_params(fetched, width)
+    by_rows = width % device_total == 0 and vectors.shape[0] <= hidden
+    if by_rows:
+        wqkv, wo, wup, wdn, vec = fetch_rows(
+            w_qkv, w_out, w_up, w_down, vectors, width, device_total
+        )
+    else:
+        wqkv, wo, wup, wdn, vec = fetch_flat(w_qkv, w_out, w_up, w_down, vectors, width)
     inputs = block_input.astype(jnp.float32)
     normed1, inverse1, pre1 = layer_norm(inputs, vec[0:width], vec[width : 2 * width])
     first = pre1.astype(jnp.bfloat16)
@@ -198,20 +264,9 @@
             jnp.sum(grad_top, axis=0),
         ]
     )
-    all_term, all_len, all_lens = shard_terms(
-        [(first, d_qkv), (mixed, d_resid_low), (second, d_upper_low), (active, out_cotangent)],
-        g_vec,
-        device_total,
-    )
-    grad_qkv, grad_out, grad_up, grad_down, grad_vectors = split_shard(
-        lax.psum_scatter(
-            all_term(jnp.int32(0), all_len * lax.axis_size("dp")),
-            "dp",
-            scatter_dimension=0,
-            tiled=True,
-        ),
-        all_lens,
-    )
+    pairs = [(first, d_qkv), (mixed, d_resid_low), (second, d_upper_low), (active, out_cotangent)]
+    reducer = reduce_rows if by_rows else reduce_flat
+    grad_qkv, grad_out, grad_up, grad_down, grad_vectors = reducer(pairs, g_vec, device_total)
     return (block_output, input_grad, grad_qkv, grad_out, grad_up, grad_down, grad_vectors)
 
 

time: 1740 us -> 742 us (0.43)
  other arithmetic: 496 us -> 27.9 us
  waiting for transfers between devices: 858 us -> 577 us
  local copies, waits for them, and re-layouts: 258 us -> 59.1 us
  blocking collectives: 42.8 us -> 0 us
    unnamed x6 -> x7, waiting for transfers between devices: 795 us -> 49.2 us
    all_gather x4 -> x0, other arithmetic: 493 us -> none  [the longest x1 156 us: body(): lax.all_gather(w_down, 'dp', axis=0, tiled=True)]
    reduce_scatter x0 -> x2, waiting for transfers between devices: none -> 306 us  [the longest x1 155 us: reduce_rows(): lax.psum_scatter(low[2].reshape(total, own, 4 * width), 'dp', scatter_dim...]
    all_gather x4 -> x3, waiting for transfers between devices: 62.7 us -> 221 us  [the longest x1 88.3 us: fetch_rows(): lax.all_gather(w_up.reshape(own, 4 * width), 'dp', axis=0, tiled=False)]
    reshape x6 -> x11, local copies, waits for them, and re-layouts: 125 us -> 50.7 us  [the longest x1 11.2 us: reduce_rows(): low[2].reshape(total, own, 4 * width)]
    dynamic_slice x4 -> x0, local copies, waits for them, and re-layouts: 69.4 us -> none  [window_term(): lax.dynamic_slice_in_dim(padded, flat_start - row_first * columns, flat_c...]
    unnamed x54 -> x34, local copies, waits for them, and re-layouts: 54.1 us -> 2.83 us
    unnamed x1 -> x0, blocking collectives: 42.8 us -> none
  transfers between devices with their start and end apart: 5 -> 6, of which waited for: 3 -> 6; matrix products, arithmetic and copies ran while one was open for 23% -> 19% of each run, Pallas kernels for 0% -> 0%
where the time goes in v1:
time: 742 us; the launch traced here: 741 us
  waiting for transfers between devices  577 us (78%)
  matrix products  62.1 us (8%)
  local copies, waits for them, and re-layouts  59.1 us (8%)
  other arithmetic  27.9 us (4%)
  between operations  14.5 us (2%)
    reduce_scatter x1, waiting for transfers between devices, reduce_rows(): lax.psum_scatter(low[2].reshape(total, own, 4 * width), 'dp', scatter_dim...  155 us
    reduce_scatter x1, waiting for transfers between devices, reduce_rows(): lax.psum_scatter(jnp.concatenate([side, extra], axis=1), 'dp', scatter_di...  152 us
    all_gather x1, waiting for transfers between devices, fetch_rows(): lax.all_gather(w_up.reshape(own, 4 * width), 'dp', axis=0, tiled=False)  88.3 us
    all_gather x1, waiting for transfers between devices, fetch_rows(): lax.all_gather(jnp.concatenate([side, extra], axis=0), 'dp', axis=0, tile...  80.3 us
    all_gather x1, waiting for transfers between devices, fetch_rows(): lax.all_gather(w_down.reshape(4 * own, width), 'dp', axis=0, tiled=True)  52.5 us
    unnamed x7, waiting for transfers between devices  49.2 us
  transfers between devices with their start and end apart: 6, of which 6 were waited for; matrix products, arithmetic and copies ran while one was open for 19% of the time, Pallas kernels for 0%

profile of v1, /device:TPU:0, one launch (start us, length us, event | category | flops | bytes accessed | tf_op | source)
XLA Modules:
  0.0 740.6 jit_solution(6020904808747366916)
XLA Ops:
  7.2 2.1 all_gather_reshape.3
  9.4 0.7 pad.8
  10.1 1.0 reshape.233
  11.1 1.2 reshape.232
  12.3 0.8 fusion.37
  13.2 1.0 reshape.243
  15.0 88.3 %all-gather.6.cloned.1.call-done = bf16[32,34,4352]{2,1,0:T(8,128)(2,1)} async-done(((bf16[1,34,4352]{2,1,0:T(8,128)(2,1)}), bf16[32,34,4352]{2,1,0:T(8,128)(2,1)}) %all-gather.6.cloned.1.call-update) | async-done | bytes 9469968 | tf_op jit(solution)/shard_map/all_gather | solution.py:135
  103.3 10.9 %reshape.242 = bf16[1088,4352]{1,0:T(8,128)(2,1)} reshape(bf16[32,34,4352]{2,1,0:T(8,128)(2,1)} %all-gather.6.cloned.1.call-done) | data formatting | bytes 18939904 | tf_op jit(solution)/shard_map/reshape | solution.py:139
  114.2 80.3 %all-gather.10.cloned.1.call-done = bf16[32,35,4352]{2,1,0:T(8,128)(2,1)} async-done(((bf16[1,35,4352]{2,1,0:T(8,128)(2,1)}), bf16[32,35,4352]{2,1,0:T(8,128)(2,1)}) %all-gather.10.cloned.1.call-update) | async-done | bytes 9748496 | tf_op jit(solution)/shard_map/all_gather | solution.py:134
  194.5 1.2 fusion.42
  195.8 10.9 %reshape.235 = bf16[1088,4352]{1,0:T(8,128)(2,1)} reshape(bf16[32,34,4352]{2,1,0:T(8,128)(2,1)} %bitcast.45) | data formatting | bytes 18939904 | tf_op jit(solution)/shard_map/reshape | solution.py:137
  206.9 6.6 fusion.4
  213.9 0.4 fusion.52
  214.8 4.4 fusion.53
  219.4 1.8 convolution_add_fusion
  221.2 1.4 copy-done
  222.6 5.3 convolution_convert_fusion
  228.2 52.5 %all-gather.8.cloned.1.call-done = bf16[4352,1088]{1,0:T(8,128)(2,1)} async-done(((bf16[136,1088]{1,0:T(8,128)(2,1)}), bf16[4352,1088]{1,0:T(8,128)(2,1)}) %all-gather.8.cloned.1.call-update) | async-done | bytes 9469968 | tf_op jit(solution)/shard_map/all_gather | solution.py:136
  280.7 7.4 %fusion.54 = (bf16[4352]{0:T(1024)(128)(2,1)S(1)}, bf16[128,4352]{1,0:T(8,128)(2,1)S(1)}) fusion(f32[128,4352]{1,0:T(8,128)} %copy-done, bf16[128,1088]{0,1:T(8,128)(2,1)} %param.9, bf16[4352,1088]{1,0:T(8,128)(2,1)} %all-gather.8.cloned.1.call-done), kind=kOutput, calls=%fused_computation.104 | convolution fusion | flops 1218277120 | bytes 13099520 | tf_op jit(solution)/shard_map/dot_general | solution.py:228
  288.1 5.5 convolution_convert_fusion.1
  293.6 11.2 %reshape.252 = bf16[32,34,4352]{2,1,0:T(8,128)(2,1)} reshape(bf16[1088,4352]{1,0:T(8,128)(2,1)} %convolution_convert_fusion.1) | data formatting | bytes 18939904 | tf_op jit(solution)/shard_map/reshape | solution.py:155
  304.8 1.2 reduce.3
  306.0 7.0 multiply_reduce_fusion.1
  313.0 0.4 fusion.48
  313.5 3.0 convolution_convert_fusion.4
  316.4 1.2 fusion.49
  317.8 0.4 multiply_reduce_fusion
  318.7 0.4 fusion.50
  319.2 0.5 convolution_convert_fusion.5
  319.7 6.2 fusion.28
  326.2 0.8 convolution_convert_fusion.3
  327.0 2.2 convolution_convert_fusion.2
  329.2 6.5 pad_maximum_fusion
  335.7 10.7 %reshape.247 = bf16[32,34,4352]{2,1,0:T(8,128)(2,1)} reshape(bf16[1088,4352]{1,0:T(8,128)(2,1)} %pad_maximum_fusion) | data formatting | bytes 18939904 | tf_op jit(solution)/shard_map/reshape | solution.py:157
  346.4 12.0 %fusion.1 = bf16[32,35,4352]{2,1,0:T(8,128)(2,1)} fusion(bf16[32,1,408]{2,1,0:T(2,128)(2,1)S(1)} %convert_element_type.131, bf16[32,34,4352]{2,1,0:T(8,128)(2,1)} %reshape.247), kind=kLoop, calls=%fused_computation.5 | loop fusion | flops 29245440 | bytes 19244544 | tf_op jit(solution)/shard_map/concatenate | solution.py:163
  358.4 1.0 copy-done.11
  359.4 1.0 fusion.27
  360.4 8.7 %fusion.8 = bf16[128,1088]{0,1:T(8,128)(2,1)} fusion(f32[128,1088]{0,1:T(8,128)S(1)} %get-tuple-element.34, bf16[4352,1088]{1,0:T(8,128)(2,1)} %all-gather.8.cloned.1.call-done, f32[1088]{0:T(1024)S(1)} %get-tuple-element.24, f32[128,4352]{1,0:T(8,128)} %copy-done), kind=kOutput, calls=%fused_computation.19 | convolution fusion | flops 1215356928 | bytes 12538112 | tf_op jit(solution)/shard_map/dot_general | solution.py:222
  369.2 49.1 %reduce-scatter.10.cloned.1.call-done = bf16[136,1088]{1,0:T(8,128)(2,1)} async-done(((bf16[4352,1088]{1,0:T(8,128)(2,1)}), bf16[136,1088]{1,0:T(8,128)(2,1)}) %reduce-scatter.10.cloned.1.call-update) | async-done | bytes 295952
  418.3 2.1 reshape.262
  420.4 154.6 %reduce-scatter.8.cloned.1.call-done = bf16[1,34,4352]{2,1,0:T(8,128)(2,1)} async-done(((bf16[32,34,4352]{2,1,0:T(8,128)(2,1)}), bf16[1,34,4352]{2,1,0:T(8,128)(2,1)}) %reduce-scatter.8.cloned.1.call-update) | async-done | bytes 295952 | tf_op jit(solution)/shard_map/reduce_scatter | solution.py:154
  575.0 2.2 reshape.260
  577.2 151.6 %reduce-scatter.6.cloned.1.call-done = bf16[1,35,4352]{2,1,0:T(8,128)(2,1)} async-done(((bf16[32,35,4352]{2,1,0:T(8,128)(2,1)}), bf16[1,35,4352]{2,1,0:T(8,128)(2,1)}) %reduce-scatter.6.cloned.1.call-update) | async-done | bytes 304656 | tf_op jit(solution)/shard_map/reduce_scatter | solution.py:162
  728.8 1.3 slice_convert_fusion.4
  730.1 1.0 slice_convert_fusion.2
  731.1 1.0 slice_convert_fusion.1
  732.1 0.8 reshape.259
  732.8 1.0 reshape.257
  (72 shorter events, 3.6 us)
Async XLA Ops:
  7.2 6.1 copy-start.12
  7.2 7.1 copy-start.13
  7.2 7.4 copy-start.1
  7.2 96.1 %all-gather.6.cloned.1.call-start = ((), (), s32[]{:S(2)}) async-start(), calls=%async_computation.3 | async-start | bytes 11489280 | tf_op jit(solution)/shard_map/all_gather | solution.py:135
  9.4 185.1 %all-gather.10.cloned.1.call-start = ((), (), s32[]{:S(2)}) async-start(), calls=%async_computation.7 | async-start | bytes 11489280 | tf_op jit(solution)/shard_map/all_gather | solution.py:134
  13.2 267.5 %all-gather.8.cloned.1.call-start = ((), (), s32[]{:S(2)}) async-start(), calls=%async_computation.4 | async-start | bytes 10340352 | tf_op jit(solution)/shard_map/all_gather | solution.py:136
  14.2 404.1 %reduce-scatter.10.cloned.1.call-start = ((), (), s32[]{:S(2)}) async-start(), calls=%async_computation.8 | async-start | bytes 10340352
  206.9 12.5 %slice-start = ((s8[9469952]{0:T(1024)(128)(4,1)}), s8[4194304]{0:T(1024)(128)(4,1)S(1)}, s32[]{:S(2)}) async-start(s8[9469952]{0:T(1024)(128)(4,1)} %bitcast.43), calls=%async_computation.9 | async-start | bytes 8388608
  206.9 12.5 %slice-start.1 = ((s8[9469952]{0:T(1024)(128)(4,1)}), s8[1081344]{0:T(1024)(128)(4,1)S(1)}, s32[]{:S(2)}) async-start(s8[9469952]{0:T(1024)(128)(4,1)} %bitcast.43), calls=%async_computation.10 | async-start | bytes 2162688
  213.5 1.0 copy-start.2
  213.8 0.9 copy-start.4
  214.2 5.2 slice-start.2
  214.8 4.6 copy-start.8
  219.4 3.2 copy-start.6
  221.2 1.4 copy-start
  228.0 347.1 %reduce-scatter.8.cloned.1.call-start = ((), (), s32[]{:S(2)}) async-start(), calls=%async_computation.6 | async-start | bytes 11489280 | tf_op jit(solution)/shard_map/reduce_scatter | solution.py:154
  304.8 424.0 %reduce-scatter.6.cloned.1.call-start = ((), (), s32[]{:S(2)}) async-start(), calls=%async_computation.5 | async-start | bytes 11489280 | tf_op jit(solution)/shard_map/reduce_scatter | solution.py:162
  306.0 7.1 copy-start.7
  313.5 4.3 copy-start.5
  317.8 1.0 copy-start.3
  318.7 1.0 copy-start.10
  319.7 6.4 copy-start.9
  358.4 1.1 copy-start.11
Sparse Core Ops, SparseCore 0:
  11.4 91.8 all-gather.5
  106.8 87.7 all-gather.9
  198.0 82.6 all-gather.7
  286.6 131.6 reduce-scatter.9
  420.5 154.5 reduce-scatter.7
  577.2 151.5 reduce-scatter.5
